TPU v7x, 128 devices: a whole 4x4x4 slice. The times are simulated.
128 devices in a mesh: shot: 32 (over x_lo, z, y), freq: 4 (over x_hi, core).
Axes of the slice: x: 4 (x_hi: 2, x_lo: 2; x = x_hi * 2 + x_lo), y: 4, z: 4, core: 2. Of those that a mesh axis runs over, the one named last changes fastest.
Arguments:
- recorded: bfloat16 [2, 256, 2048, 512], P(None, 'freq', 'shot'), may hold values from -6 to 6
- rec_shot: int32 [2048, 512], P('shot'), may hold values from 0 to 2047
- owners: int32 [3], replicated, may hold values from 0 to 31, as said below
Outputs:
- primaries: bfloat16 [2048, 512, 512], P('shot', 'freq')
- filters: float32 [2048, 31], P('shot')
Inputs may be any that keep to these rules, and one draw needn't show every extreme that they name: The 3 owners are distinct; the first and the last index of the shot axis are always among them.
All inputs are finite; a program needn't handle non-finite values.
Results may differ from a plain program's by a relative error of at most 0.008.
Values may be sent and summed in bfloat16 or wider, within the bound.
A program may use at most 192 MiB of HBM per device.

v0:
```python
import math
import jax
import jax.numpy as jnp
from jax import lax
from jax.sharding import PartitionSpec as P

F = 256
TAPS = 31
STEPS = 3
REG = 2.0


def broadcast(value, axis, source):
    kept = jnp.where(lax.axis_index(axis) == source, value, 0).astype(value.dtype)
    return lax.psum(kept, axis)


def angles(freq_index, step_index, period):
    product_mod = jnp.mod(freq_index[:, None] * step_index[None, :], period)
    return product_mod.astype(jnp.float32) * (2.0 * math.pi / period)


def solve_filters(autocorr, crosscorr, tap_count, damping):
    half_taps = (tap_count - 1) // 2
    tap_index = jnp.arange(tap_count, dtype=jnp.int32)
    distance = jnp.abs(tap_index[:, None] - tap_index[None, :])
    normal = autocorr[:, distance] + damping * jnp.eye(tap_count, dtype=jnp.float32)[None, :, :]
    target = crosscorr + damping * (tap_index == half_taps).astype(jnp.float32)[None, :]
    factor = jnp.linalg.cholesky(normal)
    middle = lax.linalg.triangular_solve(factor, target[:, :, None], left_side=True, lower=True)
    solved = lax.linalg.triangular_solve(
        factor, middle, left_side=True, lower=True, transpose_a=True
    )
    return solved[:, :, 0]


def band_table(freq_index, freq_count):
    period = 2 * freq_count
    phase_angles = angles(freq_index, jnp.arange(period, dtype=jnp.int32), period)
    norm_factor = 1.0 / math.sqrt(freq_count)
    return jnp.stack(
        [jnp.cos(phase_angles) * norm_factor, -jnp.sin(phase_angles) * norm_factor]
    ).astype(jnp.bfloat16)


def fetch_owner(data_slab, owner):
    return broadcast(data_slab, "shot", owner)


def product_step(data_slab, rec_shot, owner, owner_block):
    shot_count = data_slab.shape[2]
    offset_index = rec_shot - owner * shot_count
    slot_keys = jnp.arange(shot_count, dtype=jnp.int32)
    one_hot = (offset_index[:, None, :] == slot_keys[None, :, None]).astype(jnp.bfloat16)
    coeffs = jnp.einsum(
        "cfsr,skr->cfsk", data_slab, one_hot, preferred_element_type=jnp.float32
    ).astype(jnp.bfloat16)
    left_real = jnp.concatenate([coeffs[0], -coeffs[1]], axis=2)
    left_imag = jnp.concatenate([coeffs[1], coeffs[0]], axis=2)
    stacked = jnp.stack([left_real, left_imag])
    right_side = jnp.concatenate([owner_block[0], owner_block[1]], axis=1)
    return jnp.einsum("cfsk,fkr->cfsr", stacked, right_side, preferred_element_type=jnp.float32)


def per_device(recorded, rec_shot, owners):
    band_count = recorded.shape[1]
    recv_count = recorded.shape[3]
    half_taps = (TAPS - 1) // 2
    summed = jnp.zeros(recorded.shape, jnp.float32)
    for step_index in range(STEPS):
        owner_block = fetch_owner(recorded, owners[step_index])
        summed = summed + product_step(recorded, rec_shot, owners[step_index], owner_block)
    pred_gain = (lax.axis_size("shot") / (2.0 * recv_count * STEPS)) ** 0.5
    predicted = (pred_gain * summed).astype(jnp.bfloat16)
    pred_wide = predicted.astype(jnp.float32)
    data_wide = recorded.astype(jnp.float32)
    spectrum = jnp.sum(pred_wide[0] * pred_wide[0] + pred_wide[1] * pred_wide[1], axis=2)
    cross_real = jnp.sum(pred_wide[0] * data_wide[0] + pred_wide[1] * data_wide[1], axis=2)
    cross_imag = jnp.sum(pred_wide[0] * data_wide[1] - pred_wide[1] * data_wide[0], axis=2)
    highest = lax.Precision.HIGHEST
    freq_index = lax.axis_index("freq") * band_count + jnp.arange(band_count, dtype=jnp.int32)
    tap_index = jnp.arange(TAPS, dtype=jnp.int32)
    lag_angles = angles(freq_index, tap_index, 2 * F)
    tap_angles = angles(freq_index, tap_index - half_taps, 2 * F)
    auto_part = jnp.dot(spectrum.T, jnp.cos(lag_angles), precision=highest)
    cross_part = jnp.dot(cross_real.T, jnp.cos(tap_angles), precision=highest) - jnp.dot(
        cross_imag.T, jnp.sin(tap_angles), precision=highest
    )
    autocorr, crosscorr = lax.psum((auto_part, cross_part), "freq")
    filters = solve_filters(autocorr, crosscorr, TAPS, REG * recv_count * F)
    resp_real = jnp.dot(jnp.cos(tap_angles), filters.T, precision=highest)[:, :, None]
    resp_imag = -jnp.dot(jnp.sin(tap_angles), filters.T, precision=highest)[:, :, None]
    res_real = data_wide[0] - (resp_real * pred_wide[0] - resp_imag * pred_wide[1])
    res_imag = data_wide[1] - (resp_real * pred_wide[1] + resp_imag * pred_wide[0])
    residual = jnp.stack([res_real, res_imag]).astype(jnp.bfloat16)
    full_table = band_table(jnp.arange(F, dtype=jnp.int32), F).reshape(2 * F, 2 * F)
    shard_piece = lax.all_to_all(residual, "freq", split_axis=3, concat_axis=1, tiled=True)
    item_count = shard_piece.shape[2]
    recv_part = shard_piece.shape[3]
    flattened = shard_piece.reshape(2 * F, item_count * recv_part)
    time_rows = lax.dot_general(
        flattened, full_table, (((0,), (0,)), ((), ())), preferred_element_type=jnp.float32
    )
    primaries = time_rows.reshape(item_count, recv_part, 2 * F).astype(jnp.bfloat16)
    return (primaries, filters)


def solution(mesh):
    placed = (P(None, "freq", "shot", None), P("shot", None), P())
    return jax.shard_map(
        per_device,
        mesh=mesh,
        in_specs=placed,
        out_specs=(P("shot", "freq", None), P("shot", None)),
        check_vma=False,
    )
```

profile of v0, /device:TPU:1, one launch (start us, length us, event | category | flops | bytes accessed | tf_op | source)
XLA Modules:
  0.0 1144.3 jit_solution(10621958001166463618)
XLA Ops:
  7.2 1.4 fusion.81
  10.5 11.0 broadcast_select_fusion.1
  23.4 11.5 %copy.36 = bf16[2,64,64,512]{3,1,0,2:T(8,128)(2,1)} copy(bf16[2,64,64,512]{3,2,1,0:T(8,128)(2,1)} %param.3) | data formatting | bytes 16777216 | tf_op args[0]
  35.2 5.7 fusion.9
  40.9 0.5 convert_bitcast_fusion.2
  41.8 1.2 maximum_bitcast_fusion.10
  42.9 1.5 pad_maximum_fusion.2
  44.5 1.3 slice-done.1
  45.8 2.3 fusion.8
  48.1 0.7 convert_bitcast_fusion.3
  49.2 1.2 maximum_bitcast_fusion.8
  50.4 1.5 pad_maximum_fusion.1
  51.9 2.3 fusion.10
  54.2 0.5 convert_bitcast_fusion.1
  55.1 1.2 maximum_bitcast_fusion.12
  56.2 1.5 pad_maximum_fusion.3
  57.8 11.7 %copy_convert_fusion = f32[2,64,64,512]{3,2,0,1:T(8,128)} fusion(bf16[2,64,64,512]{3,2,1,0:T(8,128)(2,1)} %param.3), kind=kLoop, calls=%fused_computation.16 | loop fusion | flops 4194304 | bytes 25165824 | tf_op jit(solution)/shard_map/convert_element_type | solution.py:76
  69.5 510.7 %all-reduce.4.cloned.1.call-done = (bf16[2,64,64,512]{3,2,1,0:T(8,128)(2,1)}, bf16[2,64,64,512]{3,2,1,0:T(8,128)(2,1)}, bf16[2,64,64,512]{3,2,1,0:T(8,128)(2,1)}) async-done(((bf16[2,64,64,512]{3,2,1,0:T(8,128)(2,1)}, bf16[2,64,64,512]{3,2,1,0:T(8,128)(2,1)}, bf16[2,64,64,512]{3,2,1,0:T(8,128)(2,1)}), (bf16[2,64,64,512]{3,2,1,0:T(8,128)(2,1)}, bf16[2,64,64,512]{3,2,1,0:T(8,128)(2,1)}, ...) | async-done | bytes 25165840 | tf_op jit(solution)/shard_map/psum | solution.py:15
  580.2 4.0 slice_bitcast_fusion.5
  584.2 11.2 slice_bitcast_fusion.1
  595.4 10.3 fusion.3
  605.7 10.2 fusion
  615.8 20.8 %convert_bitcast_fusion = f32[2,64,64,512]{3,2,0,1:T(8,128)} fusion(bf16[64,64,512]{2,1,0:T(8,128)(2,1)} %get-tuple-element.17, bf16[64,64,512]{2,1,0:T(8,128)(2,1)S(1)} %copy-done, f32[64,512,2,64]{1,3,2,0:T(8,128)} %fusion, f32[64,512,2,64]{1,3,2,0:T(8,128)} %fusion.3, bf16[2,64,64,128]{3,1,2,0:T(8,128)(2,1)} %pad_maximum_fusion.3), kind=kOutput, calls=%fused_computation.1 | convolution fusion | flops 1111490560 | bytes 60817408 | tf_op jit(solution)/shard_map/cfsk,fkr->cfsr/dot_general | solution.py:62
  636.7 13.9 %subtract_reduce_fusion = (f32[64,64]{1,0:T(8,128)S(1)}, f32[64,64]{1,0:T(8,128)S(1)}, f32[64,64]{1,0:T(8,128)S(1)}) fusion(f32[2,64,64,512]{3,2,0,1:T(8,128)} %copy_convert_fusion, f32[2,64,64,512]{3,2,0,1:T(8,128)} %convert_bitcast_fusion), kind=kLoop, calls=%fused_computation.19 | loop fusion | flops 25153536 | bytes 33603584 | tf_op jit(solution)/shard_map/reduce_sum | solution.py:79
  650.6 0.4 fusion.33
  651.0 0.4 fusion.50
  651.4 0.4 convolution_subtract_fusion
  651.8 13.8 %all-reduce = (f32[64,31]{0,1:T(8,128)S(1)}, f32[64,31]{0,1:T(8,128)S(1)}) all-reduce(f32[64,31]{0,1:T(8,128)S(1)} %fusion.33, f32[64,31]{0,1:T(8,128)S(1)} %convolution_subtract_fusion), channel_id=1, replica_groups=mesh['shot'=32,'freq'=4] {'freq'}, use_global_device_ids=true, to_apply=%region_4.5 | all-reduce | flops 3968 | bytes 31744 | tf_op jit(solution)/shard_map/psum | solution.py:89
  665.6 2.9 gather_fusion
  668.6 1.0 copy.45
  669.5 1.0 copy.46
  670.5 1.2 fusion.18
  671.7 182.3 %custom-call.9 = f32[64,31,31]{2,1,0:T(8,128)S(1)} custom-call(f32[64,31,31]{2,1,0:T(8,128)} %fusion.18), custom_call_target="Cholesky" | custom-call | tf_op jit(solution)/shard_map/jit(cholesky)/cholesky | solution.py:29
  854.0 0.6 copy.47
  855.1 11.7 %custom-call.10 = f32[64,1,31,31]{0,2,3,1:T(8,128)S(1)} custom-call(f32[64,1,31,31]{0,3,2,1:T(8,128)S(1)} %select_bitcast_fusion), custom_call_target="InvertDiagBlocksLowerTriangular" | custom-call | tf_op jit(solution)/shard_map/triangular_solve | solution.py:31
  867.4 0.4 convolution_negate_fusion
  867.8 13.7 %subtract_convert_fusion.1 = (bf16[1,64,64,512]{3,2,0,1:T(8,128)(2,1)S(1)}, bf16[1,64,64,512]{3,2,0,1:T(8,128)(2,1)}) fusion(f32[2,64,64,512]{3,2,0,1:T(8,128)} %copy_convert_fusion, f32[2,64,64,512]{3,2,0,1:T(8,128)} %convert_bitcast_fusion, f32[64,64]{1,0:T(8,128)S(1)} %convolution_negate_fusion, f32[64,64]{1,0:T(8,128)S(1)} %fusion.48), kind=kLoop, calls=%fused_computation.18 | loop fusion | flops 20971520 | bytes 41975808 | tf_op jit(solution)/shard_map/convert.2
  881.5 6.4 pad_maximum_fusion
  887.9 34.3 %copy.49 = bf16[2,64,64,512]{2,0,1,3:T(2,128)(2,1)} copy(bf16[2,64,64,512]{3,2,0,1:T(8,128)(2,1)} %pad_maximum_fusion) | data formatting | bytes 16777216 | tf_op jit(solution)/shard_map/stack | solution.py:95
  922.2 16.6 %reshape.205 = bf16[4,2,524288]{2,1,0:T(2,128)(2,1)} reshape(bf16[512,64,2,64]{3,2,1,0:T(2,128)(2,1)} %bitcast.133) | data formatting | bytes 16777216
  938.8 8.4 all-to-all-start
  947.1 2.2 multiply_convert_fusion.1
  949.4 91.6 %all-to-all-done = bf16[4,2,524288]{2,1,0:T(2,128)(2,1)} async-done(((bf16[4,2,524288]{2,1,0:T(2,128)(2,1)}), bf16[4,2,524288]{2,1,0:T(2,128)(2,1)}, u32[]{:S(2)}, u32[]{:S(2)}) %all-to-all-start) | async-done | bytes 8388640 | tf_op jit(solution)/shard_map/all_to_all | solution.py:97
  1041.0 16.0 %reshape.206 = bf16[512,64,2,64]{3,2,1,0:T(2,128)(2,1)} reshape(bf16[4,2,524288]{2,1,0:T(2,128)(2,1)} %all-to-all-done) | data formatting | bytes 16777216
  1056.9 34.3 %copy.50 = bf16[2,64,64,4,128]{4,2,1,3,0:T(8,128)(2,1)} copy(bf16[2,64,64,4,128]{2,0,1,4,3:T(2,128)(2,1)} %bitcast.134) | data formatting | bytes 16777216 | tf_op jit(solution)/shard_map/all_to_all | solution.py:97
  1091.2 23.6 %copy.80 = bf16[64,8,64,128]{3,1,2,0:T(8,128)(2,1)} copy(bf16[64,8,64,128]{3,2,1,0:T(8,128)(2,1)} %bitcast.135) | data formatting | bytes 16777216
  1114.9 12.0 %copy.51 = bf16[8192,512]{1,0:T(8,128)(2,1)} copy(bf16[8192,512]{0,1:T(8,128)(2,1)} %bitcast.136) | data formatting | bytes 16777216 | tf_op jit(solution)/shard_map/dot_general | solution.py:101
  1126.9 10.1 convolution_convert_fusion
  (37 shorter events, 2.4 us)
Async XLA Ops:
  7.2 573.1 %all-reduce.4.cloned.1.call-start = ((), (), s32[]{:S(2)}) async-start(), calls=%async_computation.1 | async-start | bytes 50331648 | tf_op jit(solution)/shard_map/psum | solution.py:15
  23.4 11.7 %copy-start.1 = (s32[64,512]{1,0:T(8,128)S(1)}, s32[64,512]{1,0:T(8,128)}, u32[]{:S(2)}) copy-start(s32[64,512]{1,0:T(8,128)} %param.4) | copy-start | bytes 393220
  41.4 3.1 slice-start
  41.8 4.0 slice-start.1
  605.7 10.2 copy-start
  867.1 14.4 %copy-start.2 = (f32[64,31]{0,1:T(8,128)}, f32[64,31]{0,1:T(8,128)S(1)}, u32[]{:S(2)}) copy-start(f32[64,31]{0,1:T(8,128)S(1)} %fusion.26) | copy-start | bytes 23812
  938.8 102.2 %all-to-all-start = ((bf16[4,2,524288]{2,1,0:T(2,128)(2,1)}), bf16[4,2,524288]{2,1,0:T(2,128)(2,1)}, u32[]{:S(2)}, u32[]{:S(2)}) async-start(bf16[4,2,524288]{2,1,0:T(2,128)(2,1)} %reshape.205), calls=%async_computation | async-start | bytes 16777216 | tf_op jit(solution)/shard_map/all_to_all | solution.py:97
Sparse Core Ops, SparseCore 0:
  21.6 558.5 all-reduce.3
where the time goes:
time: 1160 us; the launch traced here: 1140 us
  waiting for transfers between devices  602 us (52%)
  other arithmetic  265 us (23%)
  local copies, waits for them, and re-layouts  172 us (15%)
  matrix products  63.8 us (6%)
  between operations  18.6 us (2%)
  blocking collectives  13.8 us (1%)
    psum x1, waiting for transfers between devices, broadcast(): return lax.psum(kept, axis)  511 us
    another operation x4, other arithmetic, solve_filters(): factor = jnp.linalg.cholesky(normal)  182 us
    all_to_all x1, waiting for transfers between devices, per_device(): lax.all_to_all(residual, 'freq', split_axis=3, concat_axis=1, tiled=True)  91.6 us
    unnamed x14, local copies, waits for them, and re-layouts  69.1 us
    dot_general x3, matrix products, product_step(): jnp.einsum('cfsk,fkr->cfsr', stacked, right_side, preferred_element_type=...  41.3 us
    another operation x1, local copies, waits for them, and re-layouts, per_device(): residual = jnp.stack([res_real, res_imag]).astype(jnp.bfloat16)  34.3 us
    all_to_all x1, local copies, waits for them, and re-layouts, per_device(): lax.all_to_all(residual, 'freq', split_axis=3, concat_axis=1, tiled=True)  34.3 us
  transfers between devices with their start and end apart: 2, of which 2 were waited for; matrix products, arithmetic and copies ran while one was open for 4% of the time, Pallas kernels for 0%

commit v1 on v0

--- a/solution.py
+++ b/solution.py
@@ -94,7 +94,15 @@
     res_imag = data_wide[1] - (resp_real * pred_wide[1] + resp_imag * pred_wide[0])
     residual = jnp.stack([res_real, res_imag]).astype(jnp.bfloat16)
     full_table = band_table(jnp.arange(F, dtype=jnp.int32), F).reshape(2 * F, 2 * F)
-    shard_piece = lax.all_to_all(residual, "freq", split_axis=3, concat_axis=1, tiled=True)
+    shard_piece = jnp.concatenate(
+        jax.lax.all_to_all(
+            jnp.stack(jnp.split(residual, jax.lax.psum(1, axis_name="freq"), axis=3), axis=0),
+            axis_name="freq",
+            split_axis=0,
+            concat_axis=0,
+        ),
+        axis=1,
+    )
     item_count = shard_piece.shape[2]
     recv_part = shard_piece.shape[3]
     flattened = shard_piece.reshape(2 * F, item_count * recv_part)

time: 1160 us -> 1060 us (0.914)
  local copies, waits for them, and re-layouts: 172 us -> 80.8 us
    another operation x1 -> x0, local copies, waits for them, and re-layouts: 34.3 us -> none  [per_device(): residual = jnp.stack([res_real, res_imag]).astype(jnp.bfloat16)]
    all_to_all x1 -> x0, local copies, waits for them, and re-layouts: 34.3 us -> none  [per_device(): lax.all_to_all(residual, 'freq', split_axis=3, concat_axis=1, tiled=True)]
    unnamed x14 -> x12, local copies, waits for them, and re-layouts: 69.1 us -> 36.4 us
  transfers between devices with their start and end apart: 2 -> 2, of which waited for: 2 -> 2; matrix products, arithmetic and copies ran while one was open for 4% -> 5% of each run, Pallas kernels for 0% -> 0%
where the time goes in v1:
time: 1060 us; the launch traced here: 1050 us
  waiting for transfers between devices  602 us (57%)
  other arithmetic  263 us (25%)
  local copies, waits for them, and re-layouts  80.8 us (8%)
  matrix products  63.4 us (6%)
  between operations  18.3 us (2%)
  blocking collectives  13.6 us (1%)
    psum x1, waiting for transfers between devices, broadcast(): return lax.psum(kept, axis)  511 us
    another operation x4, other arithmetic, solve_filters(): factor = jnp.linalg.cholesky(normal)  182 us
    all_to_all x1, waiting for transfers between devices, per_device(): jax.lax.all_to_all(jnp.stack(jnp.split(residual, jax.lax.psum(1, axis_nam...  91.2 us
    dot_general x3, matrix products, product_step(): jnp.einsum('cfsk,fkr->cfsr', stacked, right_side, preferred_element_type=...  41 us
    unnamed x12, local copies, waits for them, and re-layouts  36.4 us
  transfers between devices with their start and end apart: 2, of which 2 were waited for; matrix products, arithmetic and copies ran while one was open for 5% of the time, Pallas kernels for 0%

profile of v1, /device:TPU:1, one launch (start us, length us, event | category | flops | bytes accessed | tf_op | source)
XLA Modules:
  0.0 1049.0 jit_solution(16014030800375632436)
XLA Ops:
  7.2 1.4 fusion.88
  10.4 11.0 %broadcast_select_fusion.1 = (bf16[2,64,64,512]{3,2,1,0:T(8,128)(2,1)}, bf16[2,64,64,512]{3,2,1,0:T(8,128)(2,1)}, bf16[2,64,64,512]{3,2,1,0:T(8,128)(2,1)}) fusion(bf16[2,64,64,512]{3,2,1,0:T(8,128)(2,1)} %param.3, pred[]{:T(512)S(6)} %eq.69, pred[]{:T(512)S(6)} %eq.65, pred[]{:T(512)S(6)} %eq.73), kind=kLoop, calls=%fused_computation.35 | loop fusion | flops 12582912 | bytes 33554436 | tf_op jit(solution)/shard_map/jit(_where)/select_n | solution.py:14
  23.3 11.5 %copy.36 = bf16[2,64,64,512]{3,1,0,2:T(8,128)(2,1)} copy(bf16[2,64,64,512]{3,2,1,0:T(8,128)(2,1)} %param.3) | data formatting | bytes 16777216 | tf_op args[0]
  35.0 5.7 fusion.9
  40.8 0.5 convert_bitcast_fusion.2
  41.7 1.2 maximum_bitcast_fusion.10
  42.8 1.5 pad_maximum_fusion.3
  44.4 1.3 slice-done.1
  45.7 2.3 fusion.8
  48.0 1.0 convert_bitcast_fusion.3
  49.3 1.2 maximum_bitcast_fusion.8
  50.5 1.5 pad_maximum_fusion.2
  52.0 2.3 fusion.10
  54.3 0.5 convert_bitcast_fusion.1
  55.0 0.2 slice_bitcast_fusion.6
  55.2 1.2 maximum_bitcast_fusion.12
  56.4 1.5 pad_maximum_fusion.4
  57.9 11.7 %copy_convert_fusion = f32[2,64,64,512]{3,2,0,1:T(8,128)} fusion(bf16[2,64,64,512]{3,2,1,0:T(8,128)(2,1)} %param.3), kind=kLoop, calls=%fused_computation.22 | loop fusion | flops 4194304 | bytes 25165824 | tf_op jit(solution)/shard_map/convert_element_type | solution.py:76
  69.6 510.6 %all-reduce.4.cloned.1.call-done = (bf16[2,64,64,512]{3,2,1,0:T(8,128)(2,1)}, bf16[2,64,64,512]{3,2,1,0:T(8,128)(2,1)}, bf16[2,64,64,512]{3,2,1,0:T(8,128)(2,1)}) async-done(((bf16[2,64,64,512]{3,2,1,0:T(8,128)(2,1)}, bf16[2,64,64,512]{3,2,1,0:T(8,128)(2,1)}, bf16[2,64,64,512]{3,2,1,0:T(8,128)(2,1)}), (bf16[2,64,64,512]{3,2,1,0:T(8,128)(2,1)}, bf16[2,64,64,512]{3,2,1,0:T(8,128)(2,1)}, ...) | async-done | bytes 25165840 | tf_op jit(solution)/shard_map/psum | solution.py:15
  580.2 4.0 slice_bitcast_fusion.5
  584.2 11.2 %slice_bitcast_fusion.1 = (bf16[64,64,512]{2,1,0:T(8,128)(2,1)}, bf16[64,64,512]{2,1,0:T(8,128)(2,1)}, bf16[64,64,512]{2,1,0:T(8,128)(2,1)S(1)}, bf16[64,64,512]{2,1,0:T(8,128)(2,1)}) fusion(bf16[2,64,64,512]{3,2,1,0:T(8,128)(2,1)} %get-tuple-element.7, bf16[2,64,64,512]{3,2,1,0:T(8,128)(2,1)} %get-tuple-element.9), kind=kLoop, calls=%fused_computation.39 | loop fusion | bytes 33554432 | tf_op jit(solution)/shard_map/squeeze | solution.py:61
  595.3 10.3 fusion.3
  605.6 9.9 fusion
  615.5 20.8 %convert_bitcast_fusion = f32[2,64,64,512]{3,2,0,1:T(8,128)} fusion(bf16[64,64,512]{2,1,0:T(8,128)(2,1)} %get-tuple-element.21, bf16[64,64,512]{2,1,0:T(8,128)(2,1)S(1)} %copy-done, f32[64,512,2,64]{1,3,2,0:T(8,128)} %fusion, f32[64,512,2,64]{1,3,2,0:T(8,128)} %fusion.3, bf16[2,64,64,128]{3,1,2,0:T(8,128)(2,1)} %pad_maximum_fusion.4), kind=kOutput, calls=%fused_computation.1 | convolution fusion | flops 1111490560 | bytes 60817408 | tf_op jit(solution)/shard_map/cfsk,fkr->cfsr/dot_general | solution.py:62
  636.3 13.9 %subtract_reduce_fusion = (f32[64,64]{1,0:T(8,128)S(1)}, f32[64,64]{1,0:T(8,128)S(1)}, f32[64,64]{1,0:T(8,128)S(1)}) fusion(f32[2,64,64,512]{3,2,0,1:T(8,128)} %copy_convert_fusion, f32[2,64,64,512]{3,2,0,1:T(8,128)} %convert_bitcast_fusion), kind=kLoop, calls=%fused_computation.25 | loop fusion | flops 25153536 | bytes 33603584 | tf_op jit(solution)/shard_map/reduce_sum | solution.py:79
  650.2 0.4 fusion.40
  650.6 0.4 fusion.57
  651.0 0.4 convolution_subtract_fusion
  651.5 13.6 %all-reduce = (f32[64,31]{0,1:T(8,128)S(1)}, f32[64,31]{0,1:T(8,128)S(1)}) all-reduce(f32[64,31]{0,1:T(8,128)S(1)} %fusion.40, f32[64,31]{0,1:T(8,128)S(1)} %convolution_subtract_fusion), channel_id=1, replica_groups=mesh['shot'=32,'freq'=4] {'freq'}, use_global_device_ids=true, to_apply=%region_4.5 | all-reduce | flops 3968 | bytes 31744 | tf_op jit(solution)/shard_map/psum | solution.py:89
  665.0 2.9 gather_fusion
  668.0 1.0 copy.45
  668.9 1.0 copy.46
  669.9 1.2 fusion.25
  671.1 182.3 %custom-call.9 = f32[64,31,31]{2,1,0:T(8,128)S(1)} custom-call(f32[64,31,31]{2,1,0:T(8,128)} %fusion.25), custom_call_target="Cholesky" | custom-call | tf_op jit(solution)/shard_map/jit(cholesky)/cholesky | solution.py:29
  853.4 0.6 copy.47
  854.5 11.7 %custom-call.10 = f32[64,1,31,31]{0,2,3,1:T(8,128)S(1)} custom-call(f32[64,1,31,31]{0,3,2,1:T(8,128)S(1)} %select_bitcast_fusion), custom_call_target="InvertDiagBlocksLowerTriangular" | custom-call | tf_op jit(solution)/shard_map/triangular_solve | solution.py:31
  866.5 0.3 fusion.55
  866.8 0.4 convolution_negate_fusion
  867.2 11.6 %subtract_convert_fusion.1 = (bf16[1,64,64,512]{3,2,0,1:T(8,128)(2,1)S(1)}, bf16[1,64,64,512]{3,2,0,1:T(8,128)(2,1)S(1)}) fusion(f32[2,64,64,512]{3,2,0,1:T(8,128)} %copy_convert_fusion, f32[2,64,64,512]{3,2,0,1:T(8,128)} %convert_bitcast_fusion, f32[64,64]{1,0:T(8,128)S(1)} %convolution_negate_fusion, f32[64,64]{1,0:T(8,128)S(1)} %fusion.55), kind=kLoop, calls=%fused_computation.24 | loop fusion | flops 20971520 | bytes 41975808 | tf_op jit(solution)/shard_map/convert.2
  878.8 1.7 fusion.17
  880.6 3.9 pad_maximum_fusion
  884.4 8.4 all-to-all-start
  892.8 2.6 multiply_convert_fusion.1
  895.5 91.2 %all-to-all-done = bf16[4,2,64,64,128]{4,3,1,2,0:T(8,128)(2,1)} async-done(((bf16[4,2,64,64,128]{4,3,1,2,0:T(8,128)(2,1)}), bf16[4,2,64,64,128]{4,3,1,2,0:T(8,128)(2,1)}, u32[]{:S(2)}, u32[]{:S(2)}) %all-to-all-start) | async-done | bytes 8388640 | tf_op jit(solution)/shard_map/all_to_all | solution.py:98
  986.7 9.7 copy.49
  996.3 23.6 %copy.79 = bf16[64,8,64,128]{3,1,2,0:T(8,128)(2,1)} copy(bf16[64,8,64,128]{3,2,1,0:T(8,128)(2,1)} %bitcast.138) | data formatting | bytes 16777216
  1019.9 12.0 %copy.50 = bf16[8192,512]{1,0:T(8,128)(2,1)} copy(bf16[8192,512]{0,1:T(8,128)(2,1)} %bitcast.139) | data formatting | bytes 16777216 | tf_op jit(solution)/shard_map/dot_general | solution.py:109
  1031.9 10.1 convolution_convert_fusion
  (35 shorter events, 1.8 us)
Async XLA Ops:
  7.2 573.0 %all-reduce.4.cloned.1.call-start = ((), (), s32[]{:S(2)}) async-start(), calls=%async_computation.1 | async-start | bytes 50331648 | tf_op jit(solution)/shard_map/psum | solution.py:15
  23.2 11.7 %copy-start.1 = (s32[64,512]{1,0:T(8,128)S(1)}, s32[64,512]{1,0:T(8,128)}, u32[]{:S(2)}) copy-start(s32[64,512]{1,0:T(8,128)} %param.4) | copy-start | bytes 393220
  41.3 3.1 slice-start
  41.7 4.0 slice-start.1
  605.6 9.9 copy-start
  866.5 12.4 %copy-start.2 = (f32[64,31]{0,1:T(8,128)}, f32[64,31]{0,1:T(8,128)S(1)}, u32[]{:S(2)}) copy-start(f32[64,31]{0,1:T(8,128)S(1)} %fusion.33) | copy-start | bytes 23812
  884.4 102.2 %all-to-all-start = ((bf16[4,2,64,64,128]{4,3,1,2,0:T(8,128)(2,1)}), bf16[4,2,64,64,128]{4,3,1,2,0:T(8,128)(2,1)}, u32[]{:S(2)}, u32[]{:S(2)}) async-start(bf16[4,2,64,64,128]{4,3,1,2,0:T(8,128)(2,1)} %pad_maximum_fusion), calls=%async_computation | async-start | bytes 16777216 | tf_op jit(solution)/shard_map/all_to_all | solution.py:98
Sparse Core Ops, SparseCore 0:
  21.5 558.5 all-reduce.3
